TPU v7x, 32 devices: a whole 2x2x4 slice. The times are simulated.
32 devices in a mesh: facet: 8 (over z, x), stokes: 4 (over y, core).
Axes of the slice: x: 2, y: 2, z: 4, core: 2. Of those that a mesh axis runs over, the one named last changes fastest.
Arguments:
- strips: bfloat16 [4, 512, 16384], P('stokes', 'facet'), may hold values from -6 to 6
- sub_u: int32 [16], replicated, may hold values from 0 to 511
- counts: int32 [16], P('facet'), may hold values from 1 to 64, 512 in all
- uvw: int32 [3, 16, 8192], P(None, 'facet'), may hold values from 0 to 255
- mueller: float32 [4, 4, 16, 64], P(None, None, 'facet'), may hold values from -3 to 3
- observed: float32 [4, 16, 2, 8192], P('stokes', 'facet'), may hold values from -6 to 6
Outputs:
- image_out: bfloat16 [4, 512, 16384], P('stokes', 'facet')
- residual_vis: float32 [4, 16, 2, 8192], P('stokes', 'facet')
Inputs may be any that keep to these rules, and one draw needn't show every extreme that they name: Block counts of one subgrid are at most 64; some subgrid has exactly 64.
All inputs are finite; a program needn't handle non-finite values.
Results may differ from a plain program's by a relative error of at most 0.018.
Values may be sent and summed in bfloat16 or wider, within the bound.
A program may use at most 128 MiB of HBM per device.

v0:
```python
import functools
import math

import jax
import jax.numpy as jnp
import ml_dtypes
import numpy as np
from jax import lax
from jax.experimental import pallas as pl
from jax.experimental.pallas import tpu as pltpu
from jax.sharding import PartitionSpec as P

K = 64
G = 256
BLOCK = 128
PAIR = 2 * BLOCK
MESH = pl.DeviceIdType.MESH


def unit(phase, period):
    angle = phase.astype(np.float64) * (2.0 * math.pi / period)
    return np.cos(angle) + 1j * np.sin(angle)


def column_table(length):
    period = length // 4
    lpos = np.arange(period, dtype=np.int64)[:, None]
    cpos = np.arange(K, dtype=np.int64)[None, :]
    table = unit(-(4 * cpos * lpos % length), length) / math.sqrt(length)
    re, im = table.real, table.imag
    return np.concatenate([np.concatenate([re, im], 1), np.concatenate([-im, re], 1)], 0).astype(
        ml_dtypes.bfloat16
    )


def interp_table():
    upos = np.arange(G, dtype=np.int64)[:, None, None]
    kpos = np.arange(K, dtype=np.int64)[None, :, None]
    mpos = np.arange(K, dtype=np.int64)[None, None, :] - K // 2
    return unit(mpos * (upos - 4 * kpos) % G, G).sum(2) / (2.0 * K)


def lift_table(interp, nfac, rows):
    total = nfac * rows
    upos = np.arange(G, dtype=np.int64)[:, None]
    kpos = np.arange(K, dtype=np.int64)
    blocks = []
    for f in range(nfac):
        centre = f * rows + rows // 2
        e = interp * unit(4 * kpos[None, :] * centre % total - upos * centre % total, total)
        rpos = f * rows + np.arange(rows, dtype=np.int64)
        fourier = unit(-(4 * kpos[:, None] * rpos[None, :] % total), total) / math.sqrt(total)
        blocks.append(e @ fourier)
    return np.concatenate(blocks, 1)


def turn_of(n, period):
    fraction = n.astype(jnp.float32) * (4.0 / period)
    quarter = (fraction + 0.5).astype(jnp.int32)
    angle = (fraction - quarter.astype(jnp.float32)) * (0.5 * math.pi)
    x2 = angle * angle
    sin = angle * (1.0 + x2 * (-1.0 / 6 + x2 * (1.0 / 120 + x2 * (-1.0 / 5040 + x2 / 362880.0))))
    cos = 1.0 + x2 * (-0.5 + x2 * (1.0 / 24 + x2 * (-1.0 / 720 + x2 / 40320.0)))
    odd = (quarter & 1) == 1
    base_c = jnp.where(odd, sin, cos)
    base_s = jnp.where(odd, cos, sin)
    q = quarter & 3
    cosine = jnp.where((q == 1) | (q == 2), -base_c, base_c)
    sine = jnp.where(q >= 2, -base_s, base_s)
    return cosine, sine


def half_sign(shape, first):
    lane = lax.broadcasted_iota(jnp.int32, shape, 1)
    return jnp.where(lane < K, first, -first).astype(jnp.float32)


def fill_phases(offsets_ref, first, owned, ph):
    total = ph.shape[1]
    rpos = lax.broadcasted_iota(jnp.int32, ph.shape[1:], 0)
    for j in range(owned):
        product = rpos * offsets_ref[first + j]
        phase = product & (total - 1) if total & (total - 1) == 0 else lax.rem(product, total)
        cosine, sine = turn_of(phase, total)
        ph[j] = cosine
        ph[owned + j] = -sine


def entry_barrier(f, s, nfac, nst):
    barrier = pltpu.get_barrier_semaphore()
    for k in range(1, nfac):
        pl.semaphore_signal(barrier, inc=1, device_id=(lax.rem(f + k, nfac), s), device_id_type=MESH)
    for k in range(1, nst):
        pl.semaphore_signal(barrier, inc=1, device_id=(f, s ^ k), device_id_type=MESH)
    return barrier


def predict_kernel(
    nfac,
    nst,
    owned,
    strips_ref,
    column_ref,
    m0_ref,
    offsets_ref,
    obs_ref,
    yall_ref,
    obuf_ref,
    cbuf,
    ph,
    osend,
    orecv,
    csend,
    crecv,
    ysend,
    yrecv,
):
    f = lax.axis_index("facet")
    s = lax.axis_index("stokes")
    rows = strips_ref.shape[1]
    steps = obuf_ref.shape[1]
    barrier = entry_barrier(f, s, nfac, nst)
    period = column_ref.shape[0] // 2
    folded = []
    for half in range(2):
        acc = None
        for rep in range(4):
            piece = strips_ref[0, :, pl.ds((half * 4 + rep) * period, period)].astype(jnp.float32)
            acc = piece if acc is None else acc + piece
        folded.append(acc.astype(jnp.bfloat16))
    coeffs = jnp.dot(folded[0], column_ref[:period], preferred_element_type=jnp.float32)
    coeffs += jnp.dot(folded[1], column_ref[period:], preferred_element_type=jnp.float32)
    mine = pl.ds(pl.multiple_of(f * rows, rows), rows)
    cbuf[mine, :] = coeffs.astype(jnp.bfloat16)
    pl.semaphore_wait(barrier, nfac + nst - 2)
    coeff_copies = []
    for k in range(1, nfac):
        copy = pltpu.make_async_remote_copy(
            src_ref=cbuf.at[mine],
            dst_ref=cbuf.at[mine],
            send_sem=csend.at[k - 1],
            recv_sem=crecv.at[k - 1],
            device_id=(lax.rem(f + k, nfac), s),
            device_id_type=MESH,
        )
        copy.start()
        coeff_copies.append(copy)
    obs_copies = []
    for k in range(1, nst):
        peer = s ^ k
        for t in range(steps):
            copy = pltpu.make_async_remote_copy(
                src_ref=obs_ref.at[0, :, :, pl.ds(pl.multiple_of((nst * t + peer) * PAIR, PAIR), PAIR)],
                dst_ref=obuf_ref.at[s, t],
                send_sem=osend.at[k - 1, t],
                recv_sem=orecv.at[k - 1, t],
                device_id=(f, peer),
                device_id_type=MESH,
            )
            copy.start()
            obs_copies.append(copy)
    for t in range(steps):
        obuf_ref[s, t] = obs_ref[0, :, :, pl.ds(pl.multiple_of((nst * t + s) * PAIR, PAIR), PAIR)]
    fill_phases(offsets_ref, f * owned, owned, ph)
    for copy in coeff_copies:
        copy.wait_recv()
    c = cbuf[...].astype(jnp.float32)
    sign = half_sign(c.shape, -1.0)
    swapped = pltpu.roll(c, K, 1) * sign
    tops, bottoms = [], []
    for j in range(owned):
        z = c * ph[j] + swapped * ph[owned + j]
        tops.append(z.astype(jnp.bfloat16))
        bottoms.append((pltpu.roll(z, K, 1) * sign).astype(jnp.bfloat16))
    zz = jnp.concatenate([jnp.concatenate(tops, 1), jnp.concatenate(bottoms, 1)], 0)
    y = jnp.dot(m0_ref[...], zz, preferred_element_type=jnp.float32)
    yall_ref[s] = y.T.astype(jnp.bfloat16)

    def send(slot, bit, index):
        copy = pltpu.make_async_remote_copy(
            src_ref=yall_ref.at[slot],
            dst_ref=yall_ref.at[slot],
            send_sem=ysend.at[index],
            recv_sem=yrecv.at[index],
            device_id=(f, s ^ bit),
            device_id_type=MESH,
        )
        copy.start()
        return copy

    far = send(s, 2, 0)
    near = send(s, 1, 1)
    far.wait_recv()
    relay = send(s ^ 2, 1, 2)
    near.wait_recv()
    relay.wait_recv()
    for copy in obs_copies:
        copy.wait()
    for copy in coeff_copies + [far, near, relay]:
        copy.wait_send()


def visibility_kernel(
    nst, owned, counts_ref, mu_ref, yall_ref, interp_ref, uvw_ref, obs_ref, rbuf_ref, ya_ref, acc
):
    me = lax.axis_index("stokes")
    rbuf_ref[...] = jnp.zeros_like(rbuf_ref)
    acc[...] = jnp.zeros_like(acc)
    width = 2 * K
    for j in range(owned):
        count = counts_ref[j]
        pairs = (count + 1) // 2
        trips = ((pairs - me + nst - 1) // nst + 1) // 2

        def step(t, j=j, count=count):
            pair = nst * t + me
            lanes = pl.ds(pl.multiple_of(pair * PAIR, PAIR), PAIR)
            cells = lax.broadcasted_iota(jnp.int32, (G, PAIR), 0)
            pick_u = jnp.where(cells == uvw_ref[0, j : j + 1, lanes], 1.0, 0.0).astype(jnp.bfloat16)
            pick_w = jnp.where(cells == uvw_ref[1, j : j + 1, lanes], 1.0, 0.0).astype(jnp.bfloat16)
            cosine, sine = turn_of(uvw_ref[2, j : j + 1, lanes], G)
            table = jnp.concatenate(
                [yall_ref[s, j * width : (j + 1) * width, :] for s in range(nst)], 0
            )
            picked = jnp.dot(table, pick_u, preferred_element_type=jnp.float32)
            weights = jnp.dot(interp_ref[...], pick_w, preferred_element_type=jnp.float32)
            w_re, w_im = weights[:K], weights[K:]
            model = []
            for s in range(nst):
                y_re = picked[s * width : s * width + K]
                y_im = picked[s * width + K : (s + 1) * width]
                m_re = jnp.sum(y_re * w_re - y_im * w_im, axis=0, keepdims=True)
                m_im = jnp.sum(y_re * w_im + y_im * w_re, axis=0, keepdims=True)
                model.append(
                    jnp.concatenate([m_re * cosine + m_im * sine, m_im * cosine - m_re * sine], 0)
                )
            block = 2 * pair
            backs = []
            resids = []
            for h in range(2):
                cut = slice(h * BLOCK, (h + 1) * BLOCK)
                mix = [[mu_ref[c, s, j, block + h] for s in range(nst)] for c in range(nst)]
                resid = []
                for c in range(nst):
                    corr = mix[c][0] * model[0][:, cut]
                    for s in range(1, nst):
                        corr += mix[c][s] * model[s][:, cut]
                    value = obs_ref[c, t, j, :, cut] - corr
                    value = jnp.where(block + h < count, value, 0.0)
                    resid.append(value)
                back = []
                for s in range(nst):
                    total = mix[0][s] * resid[0]
                    for c in range(1, nst):
                        total += mix[c][s] * resid[c]
                    back.append(total)
                backs.append(back)
                resids.append(resid)
            for c in range(nst):
                rbuf_ref[c, t, j] = jnp.concatenate([resids[0][c], resids[1][c]], 1)
            terms = []
            for s in range(nst):
                back = jnp.concatenate([backs[0][s], backs[1][s]], 1)
                b_re, b_im = back[0:1], back[1:2]
                g_re = b_re * cosine - b_im * sine
                g_im = b_im * cosine + b_re * sine
                terms.append((g_re * w_re + g_im * w_im).astype(jnp.bfloat16))
                terms.append((g_im * w_re - g_re * w_im).astype(jnp.bfloat16))
            return lax.dot_general(
                jnp.concatenate(terms, 0),
                pick_u,
                (((1,), (1,)), ((), ())),
                preferred_element_type=jnp.float32,
            )

        def two_steps(i, carry):
            acc[j] += step(2 * i) + step(2 * i + 1)
            return carry

        lax.fori_loop(0, trips, two_steps, 0)
        for s in range(nst):
            ya_ref[s, j * width : (j + 1) * width, :] = acc[j, s * width : (s + 1) * width, :].astype(
                jnp.bfloat16
            )


def adjoint_kernel(
    nfac,
    nst,
    owned,
    ya_ref,
    rbuf_ref,
    m2_ref,
    offsets_ref,
    sums_ref,
    rout_ref,
    stage,
    ymid,
    yin,
    part,
    parts_in,
    ph,
    rsend,
    rrecv,
    ysend,
    yrecv,
    psend,
    precv,
):
    f = lax.axis_index("facet")
    s = lax.axis_index("stokes")
    rows = sums_ref.shape[0]
    width = 2 * K
    barrier = entry_barrier(f, s, nfac, nst)
    pl.semaphore_wait(barrier, nfac + nst - 2)

    def send(src, dst, bit, index):
        copy = pltpu.make_async_remote_copy(
            src_ref=src,
            dst_ref=dst,
            send_sem=ysend.at[index],
            recv_sem=yrecv.at[index],
            device_id=(f, s ^ bit),
            device_id_type=MESH,
        )
        copy.start()
        return copy

    first = send(ya_ref.at[s ^ 3], stage.at[0], 1, 0)
    second = send(ya_ref.at[s ^ 1], stage.at[1], 1, 1)
    first.wait_recv()
    ymid[...] = (ya_ref[s ^ 2].astype(jnp.float32) + stage[0].astype(jnp.float32)).astype(jnp.bfloat16)
    third = send(ymid, yin, 2, 2)
    resid_copies = []
    for k in range(1, nst):
        copy = pltpu.make_async_remote_copy(
            src_ref=rbuf_ref.at[s ^ k],
            dst_ref=rout_ref.at[s],
            send_sem=rsend.at[k - 1],
            recv_sem=rrecv.at[k - 1],
            device_id=(f, s ^ k),
            device_id_type=MESH,
        )
        copy.start()
        resid_copies.append(copy)
    rout_ref[s] = rbuf_ref[s]
    fill_phases(offsets_ref, f * owned, owned, ph)
    second.wait_recv()
    own = ya_ref[s].astype(jnp.float32) + stage[1].astype(jnp.float32)
    third.wait_recv()
    own = own + yin[...].astype(jnp.float32)
    turned = []
    for j in range(owned):
        turned.append(own[j * width + K : (j + 1) * width])
        turned.append(-own[j * width : j * width + K])
    rhs = jnp.concatenate([own, jnp.concatenate(turned, 0)], 1).astype(jnp.bfloat16)
    u = lax.dot_general(
        m2_ref[...], rhs, (((1,), (1,)), ((), ())), preferred_element_type=jnp.float32
    )
    partial = None
    for j in range(owned):
        uj = u[:, j * width : (j + 1) * width]
        term = uj * ph[j] + pltpu.roll(uj, K, 1) * half_sign(uj.shape, 1.0) * ph[owned + j]
        partial = term if partial is None else partial + term
    part[...] = partial.astype(jnp.bfloat16)
    part_copies = []
    for k in range(1, nfac):
        peer = lax.rem(f + k, nfac)
        copy = pltpu.make_async_remote_copy(
            src_ref=part.at[pl.ds(pl.multiple_of(peer * rows, rows), rows)],
            dst_ref=parts_in.at[k - 1],
            send_sem=psend.at[k - 1],
            recv_sem=precv.at[k - 1],
            device_id=(peer, s),
            device_id_type=MESH,
        )
        copy.start()
        part_copies.append(copy)
    result = part[pl.ds(pl.multiple_of(f * rows, rows), rows), :].astype(jnp.float32)
    for k, copy in enumerate(part_copies):
        copy.wait_recv()
        result += parts_in[k].astype(jnp.float32)
    sums_ref[...] = result.astype(jnp.bfloat16)
    for copy in resid_copies:
        copy.wait()
    for copy in part_copies + [first, second, third]:
        copy.wait_send()


def image_kernel(nst, owned, sums_ref, column_ref, rout_ref, image_ref, resid_ref, buf, sems):
    chunks = 4
    period = column_ref.shape[0] // 2
    size = 2 * period // chunks
    steps = rout_ref.shape[1]
    copies = []
    for i in range(chunks):
        cols = pl.ds(i * size, size)
        image = lax.dot_general(
            sums_ref[...], column_ref[cols, :], (((1,), (1,)), ((), ())), preferred_element_type=jnp.float32
        )
        buf[:, cols] = (8.0 * image).astype(jnp.bfloat16)
        half, offset = divmod(i * size, period)
        for rep in range(4):
            copy = pltpu.make_async_copy(
                buf.at[:, cols],
                image_ref.at[0, :, pl.ds((half * 4 + rep) * period + offset, size)],
                sems.at[i, rep],
            )
            copy.start()
            copies.append(copy)
    for q in range(nst):
        for t in range(steps):
            resid_ref[0, :, :, (nst * t + q) * PAIR : (nst * t + q + 1) * PAIR] = rout_ref[q, t]
    for copy in copies:
        copy.wait()


def body(strips, sub_u, counts, uvw, mueller, observed):
    nfac = lax.axis_size("facet")
    nst = lax.axis_size("stokes")
    rows = strips.shape[1]
    length = strips.shape[2] // 2
    total = rows * nfac
    owned = counts.shape[0]
    visits = uvw.shape[2]
    steps = visits // (PAIR * nst)
    wide = owned * 2 * K
    grant = min(60, 20 + total // 32) * 1024 * 1024 if total > 1024 else 20 * 1024 * 1024
    f32, bf16 = jnp.float32, jnp.bfloat16
    interp = interp_table()
    m0 = lift_table(interp, nfac, rows)
    column = jnp.asarray(column_table(length))
    interp_t = jnp.asarray(np.concatenate([interp.real.T, interp.imag.T], 0).astype(ml_dtypes.bfloat16))
    m0_wide = jnp.asarray(np.concatenate([m0.real, m0.imag], 1).astype(ml_dtypes.bfloat16))
    m0_tall = jnp.asarray(np.concatenate([m0.real.T, m0.imag.T], 1).astype(ml_dtypes.bfloat16))
    vmem = pl.BlockSpec(memory_space=pltpu.VMEM)
    smem = pl.BlockSpec(memory_space=pltpu.SMEM)
    dma = pltpu.SemaphoreType.DMA

    yall, obs = pl.pallas_call(
        functools.partial(predict_kernel, nfac, nst, owned),
        out_shape=(
            jax.ShapeDtypeStruct((nst, wide, G), bf16),
            jax.ShapeDtypeStruct((nst, steps, owned, 2, PAIR), f32),
        ),
        in_specs=[vmem, vmem, vmem, smem, vmem],
        out_specs=(vmem, vmem),
        scratch_shapes=[
            pltpu.VMEM((total, 2 * K), bf16),
            pltpu.VMEM((2 * owned, total, 2 * K), f32),
            dma((nst - 1, steps)),
            dma((nst - 1, steps)),
            dma((nfac - 1,)),
            dma((nfac - 1,)),
            dma((3,)),
            dma((3,)),
        ],
        compiler_params=pltpu.CompilerParams(
            collective_id=0, has_side_effects=True, vmem_limit_bytes=grant
        ),
        name="predict",
    )(strips, column, m0_wide, sub_u, observed)

    rbuf, ya = pl.pallas_call(
        functools.partial(visibility_kernel, nst, owned),
        out_shape=(
            jax.ShapeDtypeStruct((nst, steps, owned, 2, PAIR), f32),
            jax.ShapeDtypeStruct((nst, wide, G), bf16),
        ),
        in_specs=[smem, smem, vmem, vmem, vmem, vmem],
        out_specs=(vmem, vmem),
        scratch_shapes=[pltpu.VMEM((owned, nst * 2 * K, G), f32)],
        compiler_params=pltpu.CompilerParams(vmem_limit_bytes=grant),
        name="visibility",
    )(counts, mueller, yall, interp_t, uvw, obs)

    sums, rout = pl.pallas_call(
        functools.partial(adjoint_kernel, nfac, nst, owned),
        out_shape=(
            jax.ShapeDtypeStruct((rows, 2 * K), bf16),
            jax.ShapeDtypeStruct((nst, steps, owned, 2, PAIR), f32),
        ),
        in_specs=[vmem, vmem, vmem, smem],
        out_specs=(vmem, vmem),
        scratch_shapes=[
            pltpu.VMEM((2, wide, G), bf16),
            pltpu.VMEM((wide, G), bf16),
            pltpu.VMEM((wide, G), bf16),
            pltpu.VMEM((total, 2 * K), bf16),
            pltpu.VMEM((nfac - 1, rows, 2 * K), bf16),
            pltpu.VMEM((2 * owned, total, 2 * K), f32),
            dma((nst - 1,)),
            dma((nst - 1,)),
            dma((3,)),
            dma((3,)),
            dma((nfac - 1,)),
            dma((nfac - 1,)),
        ],
        compiler_params=pltpu.CompilerParams(
            collective_id=1, has_side_effects=True, vmem_limit_bytes=grant
        ),
        name="adjoint",
    )(ya, rbuf, m0_tall, sub_u)

    return pl.pallas_call(
        functools.partial(image_kernel, nst, owned),
        out_shape=(
            jax.ShapeDtypeStruct((1, rows, 2 * length), bf16),
            jax.ShapeDtypeStruct((1, owned, 2, visits), f32),
        ),
        in_specs=[vmem] * 3,
        out_specs=(pl.BlockSpec(memory_space=pl.ANY), vmem),
        scratch_shapes=[pltpu.VMEM((rows, length // 2), bf16), dma((4, 4))],
        compiler_params=pltpu.CompilerParams(vmem_limit_bytes=grant),
        name="image",
    )(sums, column, rout)


def solution(mesh):
    placed = (
        P("stokes", "facet", None),
        P(),
        P("facet"),
        P(None, "facet", None),
        P(None, None, "facet", None),
        P("stokes", "facet", None, None),
    )
    return jax.shard_map(
        body,
        mesh=mesh,
        in_specs=placed,
        out_specs=(P("stokes", "facet", None), P("stokes", "facet", None, None)),
        check_vma=False,
    )
```

profile of v0, /device:TPU:0, one launch (start us, length us, event | category | flops | bytes accessed | tf_op | source)
XLA Modules:
  0.0 45.7 jit_solution(631397968643479048)
XLA Ops:
  0.6 0.0 copy-start
  0.6 1.2 %copy-done = bf16[4096,128]{1,0:T(8,128)(2,1)S(1)} copy-done((bf16[4096,128]{1,0:T(8,128)(2,1)S(1)}, bf16[4096,128]{1,0:T(8,128)(2,1)}, u32[]{:S(2)}) %copy-start) | copy-done | bytes 1048600
  1.9 0.0 copy-start.1
  1.9 1.6 %copy-done.1 = bf16[1,64,16384]{2,1,0:T(8,128)(2,1)S(1)} copy-done((bf16[1,64,16384]{2,1,0:T(8,128)(2,1)S(1)}, bf16[1,64,16384]{2,1,0:T(8,128)(2,1)}, u32[]{:S(2)}) %copy-start.1) | copy-done | bytes 2097176
  3.5 0.0 copy-start.3
  3.5 1.0 %copy-done.3 = bf16[256,1024]{1,0:T(8,128)(2,1)S(1)} copy-done((bf16[256,1024]{1,0:T(8,128)(2,1)S(1)}, bf16[256,1024]{1,0:T(8,128)(2,1)}, u32[]{:S(2)}) %copy-start.3) | copy-done | bytes 524312
  4.5 0.0 copy-start.5
  4.5 0.9 %copy-done.5 = f32[1,2,2,8192]{3,2,1,0:T(2,128)S(1)} copy-done((f32[1,2,2,8192]{3,2,1,0:T(2,128)S(1)}, f32[1,2,2,8192]{3,2,1,0:T(2,128)}, u32[]{:S(2)}) %copy-start.5) | copy-done | bytes 131096
  5.4 0.0 copy-start.8
  5.4 0.7 %copy-done.8 = s32[16]{0:T(128)S(1)} copy-done((s32[16]{0:T(128)S(1)}, s32[16]{0:T(128)}, u32[]{:S(2)}) %copy-start.8) | copy-done | bytes 88
  6.1 0.0 copy-start.4
  6.1 0.0 copy-start.6
  6.1 0.0 copy-start.7
  6.1 0.0 copy-start.9
  6.1 0.0 copy-start.2
  6.1 16.5 %predict.1 = (bf16[4,256,256]{2,1,0:T(8,128)(2,1)S(1)}, f32[4,8,2,2,256]{4,3,2,1,0:T(2,128)S(1)}) custom-call(bf16[1,64,16384]{2,1,0:T(8,128)(2,1)S(1)} %copy-done.1, bf16[4096,128]{1,0:T(8,128)(2,1)S(1)} %copy-done, bf16[256,1024]{1,0:T(8,128)(2,1)S(1)} %copy-done.3, s32[16]{0:T(128)S(1)} %copy-done.8, f32[1,2,2,8192]{3,2,1,0:T(2,128)S(1)} %copy-done.5), custom_call_target="tpu_custom_call" | custom-call | tf_op jit(solution)/shard_map/predict/pallas_call | solution.py:440
  22.6 0.0 copy-done.4
  22.6 0.0 copy-done.6
  22.6 0.0 copy-done.7
  22.6 0.0 copy-done.9
  22.6 5.0 %visibility.1 = (f32[4,8,2,2,256]{4,3,2,1,0:T(2,128)S(1)}, bf16[4,256,256]{2,1,0:T(8,128)(2,1)S(1)}) custom-call(s32[2]{0:T(128)S(1)} %copy-done.9, f32[4,4,2,64]{3,2,1,0:T(2,128)S(1)} %copy-done.7, bf16[4,256,256]{2,1,0:T(8,128)(2,1)S(1)} %get-tuple-element.8.yall_ref, bf16[128,256]{1,0:T(8,128)(2,1)S(1)} %copy-done.6, s32[3,2,8192]{2,1,0:T(2,128)S(1)} %copy-done.4, ...), custom_call_target="tpu_custom_call" | custom-call | tf_op jit(solution)/shard_map/visibility/pallas_call | solution.py:464
  27.6 0.0 copy-done.2
  27.6 15.8 %adjoint.1 = (bf16[64,128]{1,0:T(8,128)(2,1)S(1)}, f32[4,8,2,2,256]{4,3,2,1,0:T(2,128)S(1)}) custom-call(bf16[4,256,256]{2,1,0:T(8,128)(2,1)S(1)} %get-tuple-element.10.ya_ref, f32[4,8,2,2,256]{4,3,2,1,0:T(2,128)S(1)} %get-tuple-element.11.rbuf_ref, bf16[512,512]{1,0:T(8,128)(2,1)S(1)} %copy-done.2, s32[16]{0:T(128)S(1)} %copy-done.8), custom_call_target="tpu_custom_call" | custom-call | tf_op jit(solution)/shard_map/adjoint/pallas_call | solution.py:477
  43.4 2.3 %image.1 = (bf16[1,64,16384]{2,1,0:T(8,128)(2,1)}, f32[1,2,2,8192]{3,2,1,0:T(2,128)}) custom-call(bf16[64,128]{1,0:T(8,128)(2,1)S(1)} %get-tuple-element.12.sums_ref, bf16[4096,128]{1,0:T(8,128)(2,1)S(1)} %copy-done, f32[4,8,2,2,256]{4,3,2,1,0:T(2,128)S(1)} %get-tuple-element.13.rout_ref), custom_call_target="tpu_custom_call" | custom-call | tf_op jit(solution)/shard_map/image/pallas_call | solution.py:505
Async XLA Ops:
  0.6 1.2 %copy-start = (bf16[4096,128]{1,0:T(8,128)(2,1)S(1)}, bf16[4096,128]{1,0:T(8,128)(2,1)}, u32[]{:S(2)}) copy-start(bf16[4096,128]{1,0:T(8,128)(2,1)} %constant.8.clone.column_ref) | copy-start | bytes 3145732
  1.9 1.6 %copy-start.1 = (bf16[1,64,16384]{2,1,0:T(8,128)(2,1)S(1)}, bf16[1,64,16384]{2,1,0:T(8,128)(2,1)}, u32[]{:S(2)}) copy-start(bf16[1,64,16384]{2,1,0:T(8,128)(2,1)} %strips_ref.1) | copy-start | bytes 6291460
  3.5 1.0 %copy-start.3 = (bf16[256,1024]{1,0:T(8,128)(2,1)S(1)}, bf16[256,1024]{1,0:T(8,128)(2,1)}, u32[]{:S(2)}) copy-start(bf16[256,1024]{1,0:T(8,128)(2,1)} %constant.10.clone.m0_ref) | copy-start | bytes 1572868
  4.5 0.9 %copy-start.5 = (f32[1,2,2,8192]{3,2,1,0:T(2,128)S(1)}, f32[1,2,2,8192]{3,2,1,0:T(2,128)}, u32[]{:S(2)}) copy-start(f32[1,2,2,8192]{3,2,1,0:T(2,128)} %obs_ref.1) | copy-start | bytes 393220
  5.4 0.7 %copy-start.8 = (s32[16]{0:T(128)S(1)}, s32[16]{0:T(128)}, u32[]{:S(2)}) copy-start(s32[16]{0:T(128)} %offsets_ref.3) | copy-start | bytes 196
  6.1 16.5 %copy-start.4 = (s32[3,2,8192]{2,1,0:T(2,128)S(1)}, s32[3,2,8192]{2,1,0:T(2,128)}, u32[]{:S(2)}) copy-start(s32[3,2,8192]{2,1,0:T(2,128)} %uvw_ref.1) | copy-start | bytes 589828
  6.1 16.5 %copy-start.6 = (bf16[128,256]{1,0:T(8,128)(2,1)S(1)}, bf16[128,256]{1,0:T(8,128)(2,1)}, u32[]{:S(2)}) copy-start(bf16[128,256]{1,0:T(8,128)(2,1)} %constant.9.clone.interp_ref) | copy-start | bytes 196612
  6.1 16.5 %copy-start.7 = (f32[4,4,2,64]{3,2,1,0:T(2,128)S(1)}, f32[4,4,2,64]{3,2,1,0:T(2,128)}, u32[]{:S(2)}) copy-start(f32[4,4,2,64]{3,2,1,0:T(2,128)} %mu_ref.1) | copy-start | bytes 24580
  6.1 16.5 %copy-start.9 = (s32[2]{0:T(128)S(1)}, s32[2]{0:T(128)}, u32[]{:S(2)}) copy-start(s32[2]{0:T(128)} %counts_ref.1) | copy-start | bytes 28
  6.1 21.5 %copy-start.2 = (bf16[512,512]{1,0:T(8,128)(2,1)S(1)}, bf16[512,512]{1,0:T(8,128)(2,1)}, u32[]{:S(2)}) copy-start(bf16[512,512]{1,0:T(8,128)(2,1)} %constant.11.clone.m2_ref) | copy-start | bytes 1572868
where the time goes:
time: 46.4 us; the launch traced here: 45.7 us
  Pallas kernels  39.6 us (85%)
  local copies, waits for them, and re-layouts  5.43 us (12%)
  between operations  0.72 us (2%)
    pallas_call x1, Pallas kernels, body(): pl.pallas_call(functools.partial(predict_kernel, nfac, nst, owned), out_s...  16.5 us
    pallas_call x1, Pallas kernels, body(): pl.pallas_call(functools.partial(adjoint_kernel, nfac, nst, owned), out_s...  15.8 us
    unnamed x20, local copies, waits for them, and re-layouts  5.43 us
    pallas_call x1, Pallas kernels, body(): pl.pallas_call(functools.partial(visibility_kernel, nst, owned), out_shap...  5 us
    pallas_call x1, Pallas kernels, body(): pl.pallas_call(functools.partial(image_kernel, nst, owned), out_shape=(ja...  2.35 us

commit v1 on v0

--- a/solution.py
+++ b/solution.py
@@ -99,15 +99,20 @@
     nfac,
     nst,
     owned,
+    strips_hbm,
+    column_hbm,
+    m0_hbm,
+    offsets_ref,
+    obs_hbm,
+    yall_ref,
+    obuf_ref,
+    ph,
     strips_ref,
     column_ref,
     m0_ref,
-    offsets_ref,
-    obs_ref,
-    yall_ref,
-    obuf_ref,
     cbuf,
-    ph,
+    lsem,
+    osem,
     osend,
     orecv,
     csend,
@@ -117,86 +122,124 @@
 ):
     f = lax.axis_index("facet")
     s = lax.axis_index("stokes")
-    rows = strips_ref.shape[1]
+    rows = strips_ref.shape[0]
     steps = obuf_ref.shape[1]
+    period = column_ref.shape[0] // 2
+    loads = []
+    for half in range(2):
+        cols = pl.ds(half * 4 * period, 4 * period)
+        cells = pl.ds(half * period, period)
+        pair = (
+            pltpu.make_async_copy(strips_hbm.at[0, :, cols], strips_ref.at[:, cols], lsem.at[2 * half]),
+            pltpu.make_async_copy(column_hbm.at[cells], column_ref.at[cells], lsem.at[2 * half + 1]),
+        )
+        for copy in pair:
+            copy.start()
+        loads.append(pair)
+    load_m0 = pltpu.make_async_copy(m0_hbm, m0_ref, lsem.at[4])
+    load_m0.start()
+
+    def seen_by(q, t):
+        return obs_hbm.at[0, :, :, pl.ds(pl.multiple_of((nst * t + q) * PAIR, PAIR), PAIR)]
+
+    own_obs = [
+        pltpu.make_async_copy(seen_by(s, t), obuf_ref.at[s, t], osem.at[t]) for t in range(steps)
+    ]
+    for copy in own_obs:
+        copy.start()
     barrier = entry_barrier(f, s, nfac, nst)
-    period = column_ref.shape[0] // 2
-    folded = []
+    coeffs = None
     for half in range(2):
-        acc = None
+        for copy in loads[half]:
+            copy.wait()
+        total = None
         for rep in range(4):
-            piece = strips_ref[0, :, pl.ds((half * 4 + rep) * period, period)].astype(jnp.float32)
-            acc = piece if acc is None else acc + piece
-        folded.append(acc.astype(jnp.bfloat16))
-    coeffs = jnp.dot(folded[0], column_ref[:period], preferred_element_type=jnp.float32)
-    coeffs += jnp.dot(folded[1], column_ref[period:], preferred_element_type=jnp.float32)
-    mine = pl.ds(pl.multiple_of(f * rows, rows), rows)
-    cbuf[mine, :] = coeffs.astype(jnp.bfloat16)
+            piece = strips_ref[:, pl.ds((half * 4 + rep) * period, period)].astype(jnp.float32)
+            total = piece if total is None else total + piece
+        term = jnp.dot(
+            total.astype(jnp.bfloat16),
+            column_ref[pl.ds(half * period, period)],
+            preferred_element_type=jnp.float32,
+        )
+        coeffs = term if coeffs is None else coeffs + term
+
+    def rows_of(owner):
+        return pl.ds(pl.multiple_of(owner * rows, rows), rows)
+
+    cbuf[s, rows_of(f), :] = coeffs.astype(jnp.bfloat16)
     pl.semaphore_wait(barrier, nfac + nst - 2)
-    coeff_copies = []
-    for k in range(1, nfac):
+    started = []
+
+    def push(plane, owner, device, send_sem, recv_sem):
         copy = pltpu.make_async_remote_copy(
-            src_ref=cbuf.at[mine],
-            dst_ref=cbuf.at[mine],
-            send_sem=csend.at[k - 1],
-            recv_sem=crecv.at[k - 1],
-            device_id=(lax.rem(f + k, nfac), s),
+            src_ref=cbuf.at[plane, rows_of(owner)],
+            dst_ref=cbuf.at[plane, rows_of(owner)],
+            send_sem=send_sem,
+            recv_sem=recv_sem,
+            device_id=device,
             device_id_type=MESH,
         )
         copy.start()
-        coeff_copies.append(copy)
+        started.append(copy)
+        return copy
+
+    coeff_copies = [None] * nfac
+    for k in range(nfac - 1, 0, -1):
+        coeff_copies[k] = push(s, f, (f ^ k, s), csend.at[k - 1], crecv.at[k - 1])
+    far, near, relay = [], [], []
+
+    def forward(k):
+        far.append(push(s, f ^ k, (f, s ^ 2), ysend.at[0, k], yrecv.at[0, k]))
+        near.append(push(s, f ^ k, (f, s ^ 1), ysend.at[1, k], yrecv.at[1, k]))
+
+    forward(0)
     obs_copies = []
     for k in range(1, nst):
-        peer = s ^ k
         for t in range(steps):
             copy = pltpu.make_async_remote_copy(
-                src_ref=obs_ref.at[0, :, :, pl.ds(pl.multiple_of((nst * t + peer) * PAIR, PAIR), PAIR)],
+                src_ref=seen_by(s ^ k, t),
                 dst_ref=obuf_ref.at[s, t],
                 send_sem=osend.at[k - 1, t],
                 recv_sem=orecv.at[k - 1, t],
-                device_id=(f, peer),
+                device_id=(f, s ^ k),
                 device_id_type=MESH,
             )
-            copy.start()
             obs_copies.append(copy)
-    for t in range(steps):
-        obuf_ref[s, t] = obs_ref[0, :, :, pl.ds(pl.multiple_of((nst * t + s) * PAIR, PAIR), PAIR)]
     fill_phases(offsets_ref, f * owned, owned, ph)
-    for copy in coeff_copies:
+    for k in range(1, nfac):
+        coeff_copies[k].wait_recv()
+        forward(k)
+    for copy in obs_copies:
+        copy.start()
+    load_m0.wait()
+
+    def lift(plane):
+        c = cbuf[plane].astype(jnp.float32)
+        sign = half_sign(c.shape, -1.0)
+        swapped = pltpu.roll(c, K, 1) * sign
+        tops, bottoms = [], []
+        for j in range(owned):
+            z = c * ph[j] + swapped * ph[owned + j]
+            tops.append(z.astype(jnp.bfloat16))
+            bottoms.append((pltpu.roll(z, K, 1) * sign).astype(jnp.bfloat16))
+        zz = jnp.concatenate([jnp.concatenate(tops, 1), jnp.concatenate(bottoms, 1)], 0)
+        y = jnp.dot(m0_ref[...], zz, preferred_element_type=jnp.float32)
+        yall_ref[plane] = y.T.astype(jnp.bfloat16)
+
+    lift(s)
+    for k in range(nfac):
+        far[k].wait_recv()
+        relay.append(push(s ^ 2, f ^ k, (f, s ^ 1), ysend.at[2, k], yrecv.at[2, k]))
+    for copy in near:
         copy.wait_recv()
-    c = cbuf[...].astype(jnp.float32)
-    sign = half_sign(c.shape, -1.0)
-    swapped = pltpu.roll(c, K, 1) * sign
-    tops, bottoms = [], []
-    for j in range(owned):
-        z = c * ph[j] + swapped * ph[owned + j]
-        tops.append(z.astype(jnp.bfloat16))
-        bottoms.append((pltpu.roll(z, K, 1) * sign).astype(jnp.bfloat16))
-    zz = jnp.concatenate([jnp.concatenate(tops, 1), jnp.concatenate(bottoms, 1)], 0)
-    y = jnp.dot(m0_ref[...], zz, preferred_element_type=jnp.float32)
-    yall_ref[s] = y.T.astype(jnp.bfloat16)
-
-    def send(slot, bit, index):
-        copy = pltpu.make_async_remote_copy(
-            src_ref=yall_ref.at[slot],
-            dst_ref=yall_ref.at[slot],
-            send_sem=ysend.at[index],
-            recv_sem=yrecv.at[index],
-            device_id=(f, s ^ bit),
-            device_id_type=MESH,
-        )
-        copy.start()
-        return copy
-
-    far = send(s, 2, 0)
-    near = send(s, 1, 1)
-    far.wait_recv()
-    relay = send(s ^ 2, 1, 2)
-    near.wait_recv()
-    relay.wait_recv()
-    for copy in obs_copies:
+    lift(s ^ 2)
+    lift(s ^ 1)
+    for copy in relay:
+        copy.wait_recv()
+    lift(s ^ 3)
+    for copy in own_obs + obs_copies:
         copy.wait()
-    for copy in coeff_copies + [far, near, relay]:
+    for copy in started:
         copy.wait_send()
 
 
@@ -291,7 +334,7 @@
     ya_ref,
     rbuf_ref,
     m2_ref,
-    offsets_ref,
+    ph,
     sums_ref,
     rout_ref,
     stage,
@@ -299,7 +342,6 @@
     yin,
     part,
     parts_in,
-    ph,
     rsend,
     rrecv,
     ysend,
@@ -344,7 +386,6 @@
         copy.start()
         resid_copies.append(copy)
     rout_ref[s] = rbuf_ref[s]
-    fill_phases(offsets_ref, f * owned, owned, ph)
     second.wait_recv()
     own = ya_ref[s].astype(jnp.float32) + stage[1].astype(jnp.float32)
     third.wait_recv()
@@ -434,32 +475,41 @@
     m0_wide = jnp.asarray(np.concatenate([m0.real, m0.imag], 1).astype(ml_dtypes.bfloat16))
     m0_tall = jnp.asarray(np.concatenate([m0.real.T, m0.imag.T], 1).astype(ml_dtypes.bfloat16))
     vmem = pl.BlockSpec(memory_space=pltpu.VMEM)
+    hbm = pl.BlockSpec(memory_space=pltpu.HBM)
     smem = pl.BlockSpec(memory_space=pltpu.SMEM)
     dma = pltpu.SemaphoreType.DMA
 
-    yall, obs = pl.pallas_call(
+    def in_hbm(array):
+        return pltpu.with_memory_space_constraint(array, pltpu.HBM)
+
+    yall, obs, ph = pl.pallas_call(
         functools.partial(predict_kernel, nfac, nst, owned),
         out_shape=(
             jax.ShapeDtypeStruct((nst, wide, G), bf16),
             jax.ShapeDtypeStruct((nst, steps, owned, 2, PAIR), f32),
+            jax.ShapeDtypeStruct((2 * owned, total, 2 * K), f32),
         ),
-        in_specs=[vmem, vmem, vmem, smem, vmem],
-        out_specs=(vmem, vmem),
+        in_specs=[hbm, hbm, hbm, smem, hbm],
+        out_specs=(vmem, vmem, vmem),
         scratch_shapes=[
-            pltpu.VMEM((total, 2 * K), bf16),
-            pltpu.VMEM((2 * owned, total, 2 * K), f32),
+            pltpu.VMEM((rows, 2 * length), bf16),
+            pltpu.VMEM(column.shape, bf16),
+            pltpu.VMEM(m0_wide.shape, bf16),
+            pltpu.VMEM((nst, total, 2 * K), bf16),
+            dma((5,)),
+            dma((steps,)),
             dma((nst - 1, steps)),
             dma((nst - 1, steps)),
             dma((nfac - 1,)),
             dma((nfac - 1,)),
-            dma((3,)),
-            dma((3,)),
+            dma((3, nfac)),
+            dma((3, nfac)),
         ],
         compiler_params=pltpu.CompilerParams(
             collective_id=0, has_side_effects=True, vmem_limit_bytes=grant
         ),
         name="predict",
-    )(strips, column, m0_wide, sub_u, observed)
+    )(in_hbm(strips), in_hbm(column), in_hbm(m0_wide), in_hbm(sub_u), in_hbm(observed))
 
     rbuf, ya = pl.pallas_call(
         functools.partial(visibility_kernel, nst, owned),
@@ -480,7 +530,7 @@
             jax.ShapeDtypeStruct((rows, 2 * K), bf16),
             jax.ShapeDtypeStruct((nst, steps, owned, 2, PAIR), f32),
         ),
-        in_specs=[vmem, vmem, vmem, smem],
+        in_specs=[vmem] * 4,
         out_specs=(vmem, vmem),
         scratch_shapes=[
             pltpu.VMEM((2, wide, G), bf16),
@@ -488,7 +538,6 @@
             pltpu.VMEM((wide, G), bf16),
             pltpu.VMEM((total, 2 * K), bf16),
             pltpu.VMEM((nfac - 1, rows, 2 * K), bf16),
-            pltpu.VMEM((2 * owned, total, 2 * K), f32),
             dma((nst - 1,)),
             dma((nst - 1,)),
             dma((3,)),
@@ -500,7 +549,7 @@
             collective_id=1, has_side_effects=True, vmem_limit_bytes=grant
         ),
         name="adjoint",
-    )(ya, rbuf, m0_tall, sub_u)
+    )(ya, rbuf, m0_tall, ph)
 
     return pl.pallas_call(
         functools.partial(image_kernel, nst, owned),

time: 46.4 us -> 40.2 us (0.87); the launches traced: 45.7 us -> 40.5 us
  local copies, waits for them, and re-layouts: 5.43 us -> 0.03 us
    unnamed x20 -> x12, local copies, waits for them, and re-layouts: 5.43 us -> 0.03 us
    pallas_call x1, Pallas kernels: 15.8 us -> 13 us  [body(): pl.pallas_call(functools.partial(adjoint_kernel, nfac, nst, owned), out_s...]
    pallas_call x1, Pallas kernels: 5 us -> 6.64 us  [body(): pl.pallas_call(functools.partial(visibility_kernel, nst, owned), out_shap...]
    pallas_call x1, Pallas kernels: 16.5 us -> 17.8 us  [body(): pl.pallas_call(functools.partial(predict_kernel, nfac, nst, owned), out_s...]
where the time goes in v1:
time: 40.2 us; the launch traced here: 40.5 us
  Pallas kernels  39.8 us (99%)
  between operations  0.75 us (2%)
    pallas_call x1, Pallas kernels, body(): pl.pallas_call(functools.partial(predict_kernel, nfac, nst, owned), out_s...  17.8 us
    pallas_call x1, Pallas kernels, body(): pl.pallas_call(functools.partial(adjoint_kernel, nfac, nst, owned), out_s...  13 us
    pallas_call x1, Pallas kernels, body(): pl.pallas_call(functools.partial(visibility_kernel, nst, owned), out_shap...  6.64 us
    pallas_call x1, Pallas kernels, body(): pl.pallas_call(functools.partial(image_kernel, nst, owned), out_shape=(ja...  2.35 us

profile of v1, /device:TPU:0, one launch (start us, length us, event | category | flops | bytes accessed | tf_op | source)
XLA Modules:
  0.0 40.5 jit_solution(2306876816667283080)
XLA Ops:
  0.6 0.0 copy-start.3
  0.6 0.0 copy-start.1
  0.7 0.0 copy-start.4
  0.7 0.0 copy-start.2
  0.7 0.0 copy-start.5
  0.7 17.8 %predict.1 = (bf16[4,256,256]{2,1,0:T(8,128)(2,1)S(1)}, f32[4,8,2,2,256]{4,3,2,1,0:T(2,128)S(1)}, f32[4,512,128]{2,1,0:T(8,128)S(1)}) custom-call(bf16[1,64,16384]{2,1,0:T(8,128)(2,1)} %strips_hbm.1, bf16[4096,128]{1,0:T(8,128)(2,1)} %constant.8.clone.column_hbm.column_ref, bf16[256,1024]{1,0:T(8,128)(2,1)} %constant.10.clone.m0_hbm, s32[16]{0:T(128)} %offsets_ref.1, ...), custom_call_target="tpu_custom_call" | custom-call | tf_op jit(solution)/shard_map/predict/pallas_call | solution.py:485
  18.5 0.0 copy-start
  18.5 0.0 copy-done.3
  18.5 0.0 copy-done.4
  18.5 0.0 copy-done.2
  18.5 0.0 copy-done.5
  18.5 6.6 %visibility.1 = (f32[4,8,2,2,256]{4,3,2,1,0:T(2,128)S(1)}, bf16[4,256,256]{2,1,0:T(8,128)(2,1)S(1)}) custom-call(s32[2]{0:T(128)S(1)} %copy-done.5, f32[4,4,2,64]{3,2,1,0:T(2,128)S(1)} %copy-done.4, bf16[4,256,256]{2,1,0:T(8,128)(2,1)S(1)} %get-tuple-element.9.yall_ref, bf16[128,256]{1,0:T(8,128)(2,1)S(1)} %copy-done.3, s32[3,2,8192]{2,1,0:T(2,128)S(1)} %copy-done.2, ...), custom_call_target="tpu_custom_call" | custom-call | tf_op jit(solution)/shard_map/visibility/pallas_call | solution.py:514
  25.2 0.0 copy-done.1
  25.2 13.0 %adjoint.1 = (bf16[64,128]{1,0:T(8,128)(2,1)S(1)}, f32[4,8,2,2,256]{4,3,2,1,0:T(2,128)S(1)}) custom-call(bf16[4,256,256]{2,1,0:T(8,128)(2,1)S(1)} %get-tuple-element.11.ya_ref, f32[4,8,2,2,256]{4,3,2,1,0:T(2,128)S(1)} %get-tuple-element.12.rbuf_ref, bf16[512,512]{1,0:T(8,128)(2,1)S(1)} %copy-done.1, f32[4,512,128]{2,1,0:T(8,128)S(1)} %get-tuple-element.13.ph), custom_call_target="tpu_custom_call" | custom-call | tf_op jit(solution)/shard_map/adjoint/pallas_call | solution.py:527
  38.2 0.0 copy-done
  38.2 2.3 %image.1 = (bf16[1,64,16384]{2,1,0:T(8,128)(2,1)}, f32[1,2,2,8192]{3,2,1,0:T(2,128)}) custom-call(bf16[64,128]{1,0:T(8,128)(2,1)S(1)} %get-tuple-element.14.sums_ref, bf16[4096,128]{1,0:T(8,128)(2,1)S(1)} %copy-done, f32[4,8,2,2,256]{4,3,2,1,0:T(2,128)S(1)} %get-tuple-element.15.rout_ref), custom_call_target="tpu_custom_call" | custom-call | tf_op jit(solution)/shard_map/image/pallas_call | solution.py:554
Async XLA Ops:
  0.6 17.9 %copy-start.3 = (bf16[128,256]{1,0:T(8,128)(2,1)S(1)}, bf16[128,256]{1,0:T(8,128)(2,1)}, u32[]{:S(2)}) copy-start(bf16[128,256]{1,0:T(8,128)(2,1)} %constant.9.clone.interp_ref) | copy-start | bytes 196612
  0.6 24.5 %copy-start.1 = (bf16[512,512]{1,0:T(8,128)(2,1)S(1)}, bf16[512,512]{1,0:T(8,128)(2,1)}, u32[]{:S(2)}) copy-start(bf16[512,512]{1,0:T(8,128)(2,1)} %constant.11.clone.m2_ref) | copy-start | bytes 1572868
  0.7 17.8 %copy-start.4 = (f32[4,4,2,64]{3,2,1,0:T(2,128)S(1)}, f32[4,4,2,64]{3,2,1,0:T(2,128)}, u32[]{:S(2)}) copy-start(f32[4,4,2,64]{3,2,1,0:T(2,128)} %mu_ref.1) | copy-start | bytes 24580
  0.7 17.8 %copy-start.2 = (s32[3,2,8192]{2,1,0:T(2,128)S(1)}, s32[3,2,8192]{2,1,0:T(2,128)}, u32[]{:S(2)}) copy-start(s32[3,2,8192]{2,1,0:T(2,128)} %uvw_ref.1) | copy-start | bytes 589828
  0.7 17.8 %copy-start.5 = (s32[2]{0:T(128)S(1)}, s32[2]{0:T(128)}, u32[]{:S(2)}) copy-start(s32[2]{0:T(128)} %counts_ref.1) | copy-start | bytes 28
  18.5 19.7 %copy-start = (bf16[4096,128]{1,0:T(8,128)(2,1)S(1)}, bf16[4096,128]{1,0:T(8,128)(2,1)}, u32[]{:S(2)}) copy-start(bf16[4096,128]{1,0:T(8,128)(2,1)} %constant.8.clone.column_hbm.column_ref) | copy-start | bytes 3145732

commit v2 on v1

--- a/solution.py
+++ b/solution.py
@@ -337,13 +337,16 @@
     ph,
     sums_ref,
     rout_ref,
+    part,
     stage,
     ymid,
     yin,
-    part,
+    psum,
     parts_in,
     rsend,
     rrecv,
+    xsend,
+    xrecv,
     ysend,
     yrecv,
     psend,
@@ -354,77 +357,89 @@
     rows = sums_ref.shape[0]
     width = 2 * K
     barrier = entry_barrier(f, s, nfac, nst)
-    pl.semaphore_wait(barrier, nfac + nst - 2)
-
-    def send(src, dst, bit, index):
+
+    def project(plane):
+        own = ya_ref[plane]
+        turned = []
+        for j in range(owned):
+            turned.append(own[j * width + K : (j + 1) * width])
+            turned.append(-own[j * width : j * width + K])
+        rhs = jnp.concatenate([own, jnp.concatenate(turned, 0)], 1)
+        u = lax.dot_general(
+            m2_ref[...], rhs, (((1,), (1,)), ((), ())), preferred_element_type=jnp.float32
+        )
+        partial, cross = None, None
+        for j in range(owned):
+            uj = u[:, j * width : (j + 1) * width]
+            straight, crossed = uj * ph[j], pltpu.roll(uj, K, 1) * ph[owned + j]
+            partial = straight if partial is None else partial + straight
+            cross = crossed if cross is None else cross + crossed
+        part[plane] = (partial + cross * half_sign(cross.shape, 1.0)).astype(jnp.bfloat16)
+
+    def exchange(src, dst, send_sem, recv_sem, device):
         copy = pltpu.make_async_remote_copy(
             src_ref=src,
             dst_ref=dst,
-            send_sem=ysend.at[index],
-            recv_sem=yrecv.at[index],
-            device_id=(f, s ^ bit),
+            send_sem=send_sem,
+            recv_sem=recv_sem,
+            device_id=device,
             device_id_type=MESH,
         )
         copy.start()
         return copy
 
-    first = send(ya_ref.at[s ^ 3], stage.at[0], 1, 0)
-    second = send(ya_ref.at[s ^ 1], stage.at[1], 1, 1)
+    def rows_of(k):
+        return pl.ds(pl.multiple_of((f ^ k) * rows, rows), rows)
+
+    project(s ^ 3)
+    pl.semaphore_wait(barrier, nfac + nst - 2)
+    first = exchange(part.at[s ^ 3], stage.at[0], xsend.at[0], xrecv.at[0], (f, s ^ 1))
+    project(s ^ 2)
     first.wait_recv()
-    ymid[...] = (ya_ref[s ^ 2].astype(jnp.float32) + stage[0].astype(jnp.float32)).astype(jnp.bfloat16)
-    third = send(ymid, yin, 2, 2)
+    far_first = list(range(nfac - 1, -1, -1))
+    mids = {}
+    for k in far_first:
+        here = rows_of(k)
+        ymid[here, :] = (
+            part[s ^ 2, here, :].astype(jnp.float32) + stage[0, here, :].astype(jnp.float32)
+        ).astype(jnp.bfloat16)
+        mids[k] = exchange(ymid.at[here], yin.at[here], ysend.at[k], yrecv.at[k], (f, s ^ 2))
+    project(s ^ 1)
+    second = exchange(part.at[s ^ 1], stage.at[1], xsend.at[1], xrecv.at[1], (f, s ^ 1))
+    project(s)
     resid_copies = []
     for k in range(1, nst):
-        copy = pltpu.make_async_remote_copy(
-            src_ref=rbuf_ref.at[s ^ k],
-            dst_ref=rout_ref.at[s],
-            send_sem=rsend.at[k - 1],
-            recv_sem=rrecv.at[k - 1],
-            device_id=(f, s ^ k),
-            device_id_type=MESH,
-        )
-        copy.start()
-        resid_copies.append(copy)
+        resid_copies.append(
+            exchange(
+                rbuf_ref.at[s ^ k], rout_ref.at[s], rsend.at[k - 1], rrecv.at[k - 1], (f, s ^ k)
+            )
+        )
+    second.wait_recv()
+    part_copies = {}
+    result = None
+    for k in far_first:
+        here = rows_of(k)
+        mids[k].wait_recv()
+        value = (
+            part[s, here, :].astype(jnp.float32)
+            + stage[1, here, :].astype(jnp.float32)
+            + yin[here, :].astype(jnp.float32)
+        )
+        if k == 0:
+            result = value
+        else:
+            psum[here, :] = value.astype(jnp.bfloat16)
+            part_copies[k] = exchange(
+                psum.at[here], parts_in.at[k - 1], psend.at[k - 1], precv.at[k - 1], (f ^ k, s)
+            )
     rout_ref[s] = rbuf_ref[s]
-    second.wait_recv()
-    own = ya_ref[s].astype(jnp.float32) + stage[1].astype(jnp.float32)
-    third.wait_recv()
-    own = own + yin[...].astype(jnp.float32)
-    turned = []
-    for j in range(owned):
-        turned.append(own[j * width + K : (j + 1) * width])
-        turned.append(-own[j * width : j * width + K])
-    rhs = jnp.concatenate([own, jnp.concatenate(turned, 0)], 1).astype(jnp.bfloat16)
-    u = lax.dot_general(
-        m2_ref[...], rhs, (((1,), (1,)), ((), ())), preferred_element_type=jnp.float32
-    )
-    partial = None
-    for j in range(owned):
-        uj = u[:, j * width : (j + 1) * width]
-        term = uj * ph[j] + pltpu.roll(uj, K, 1) * half_sign(uj.shape, 1.0) * ph[owned + j]
-        partial = term if partial is None else partial + term
-    part[...] = partial.astype(jnp.bfloat16)
-    part_copies = []
     for k in range(1, nfac):
-        peer = lax.rem(f + k, nfac)
-        copy = pltpu.make_async_remote_copy(
-            src_ref=part.at[pl.ds(pl.multiple_of(peer * rows, rows), rows)],
-            dst_ref=parts_in.at[k - 1],
-            send_sem=psend.at[k - 1],
-            recv_sem=precv.at[k - 1],
-            device_id=(peer, s),
-            device_id_type=MESH,
-        )
-        copy.start()
-        part_copies.append(copy)
-    result = part[pl.ds(pl.multiple_of(f * rows, rows), rows), :].astype(jnp.float32)
-    for k, copy in enumerate(part_copies):
-        copy.wait_recv()
-        result += parts_in[k].astype(jnp.float32)
+        part_copies[k].wait_recv()
+        result += parts_in[k - 1].astype(jnp.float32)
     sums_ref[...] = result.astype(jnp.bfloat16)
     for copy in resid_copies:
         copy.wait()
-    for copy in part_copies + [first, second, third]:
+    for copy in [first, second] + [mids[k] for k in far_first] + list(part_copies.values()):
         copy.wait_send()
 
 
@@ -533,15 +548,18 @@
         in_specs=[vmem] * 4,
         out_specs=(vmem, vmem),
         scratch_shapes=[
-            pltpu.VMEM((2, wide, G), bf16),
-            pltpu.VMEM((wide, G), bf16),
-            pltpu.VMEM((wide, G), bf16),
+            pltpu.VMEM((nst, total, 2 * K), bf16),
+            pltpu.VMEM((2, total, 2 * K), bf16),
+            pltpu.VMEM((total, 2 * K), bf16),
+            pltpu.VMEM((total, 2 * K), bf16),
             pltpu.VMEM((total, 2 * K), bf16),
             pltpu.VMEM((nfac - 1, rows, 2 * K), bf16),
             dma((nst - 1,)),
             dma((nst - 1,)),
-            dma((3,)),
-            dma((3,)),
+            dma((2,)),
+            dma((2,)),
+            dma((nfac,)),
+            dma((nfac,)),
             dma((nfac - 1,)),
             dma((nfac - 1,)),
         ],

time: 40.2 us -> 37.7 us (0.938); the launches traced: 40.5 us -> 37.2 us
  Pallas kernels: 39.8 us -> 36.4 us
    pallas_call x1, Pallas kernels: 13 us -> 11.3 us  [body(): pl.pallas_call(functools.partial(adjoint_kernel, nfac, nst, owned), out_s...]
    pallas_call x1, Pallas kernels: 6.64 us -> 5.02 us  [body(): pl.pallas_call(functools.partial(visibility_kernel, nst, owned), out_shap...]
where the time goes in v2:
time: 37.7 us; the launch traced here: 37.2 us
  Pallas kernels  36.4 us (97%)
  between operations  0.75 us (2%)
    pallas_call x1, Pallas kernels, body(): pl.pallas_call(functools.partial(predict_kernel, nfac, nst, owned), out_s...  17.8 us
    pallas_call x1, Pallas kernels, body(): pl.pallas_call(functools.partial(adjoint_kernel, nfac, nst, owned), out_s...  11.3 us
    pallas_call x1, Pallas kernels, body(): pl.pallas_call(functools.partial(visibility_kernel, nst, owned), out_shap...  5.02 us
    pallas_call x1, Pallas kernels, body(): pl.pallas_call(functools.partial(image_kernel, nst, owned), out_shape=(ja...  2.35 us

profile of v2, /device:TPU:0, one launch (start us, length us, event | category | flops | bytes accessed | tf_op | source)
XLA Modules:
  0.0 37.2 jit_solution(9595082633382283136)
XLA Ops:
  0.6 0.0 copy-start.3
  0.6 0.0 copy-start.1
  0.7 0.0 copy-start.4
  0.7 0.0 copy-start.2
  0.7 0.0 copy-start.5
  0.7 17.8 %predict.1 = (bf16[4,256,256]{2,1,0:T(8,128)(2,1)S(1)}, f32[4,8,2,2,256]{4,3,2,1,0:T(2,128)S(1)}, f32[4,512,128]{2,1,0:T(8,128)S(1)}) custom-call(bf16[1,64,16384]{2,1,0:T(8,128)(2,1)} %strips_hbm.1, bf16[4096,128]{1,0:T(8,128)(2,1)} %constant.8.clone.column_hbm.column_ref, bf16[256,1024]{1,0:T(8,128)(2,1)} %constant.10.clone.m0_hbm, s32[16]{0:T(128)} %offsets_ref.1, ...), custom_call_target="tpu_custom_call" | custom-call | tf_op jit(solution)/shard_map/predict/pallas_call | solution.py:500
  18.5 0.0 copy-start
  18.5 0.0 copy-done.3
  18.5 0.0 copy-done.4
  18.5 0.0 copy-done.2
  18.5 0.0 copy-done.5
  18.5 5.0 %visibility.1 = (f32[4,8,2,2,256]{4,3,2,1,0:T(2,128)S(1)}, bf16[4,256,256]{2,1,0:T(8,128)(2,1)S(1)}) custom-call(s32[2]{0:T(128)S(1)} %copy-done.5, f32[4,4,2,64]{3,2,1,0:T(2,128)S(1)} %copy-done.4, bf16[4,256,256]{2,1,0:T(8,128)(2,1)S(1)} %get-tuple-element.9.yall_ref, bf16[128,256]{1,0:T(8,128)(2,1)S(1)} %copy-done.3, s32[3,2,8192]{2,1,0:T(2,128)S(1)} %copy-done.2, ...), custom_call_target="tpu_custom_call" | custom-call | tf_op jit(solution)/shard_map/visibility/pallas_call | solution.py:529
  23.6 0.0 copy-done.1
  23.6 11.3 %adjoint.1 = (bf16[64,128]{1,0:T(8,128)(2,1)S(1)}, f32[4,8,2,2,256]{4,3,2,1,0:T(2,128)S(1)}) custom-call(bf16[4,256,256]{2,1,0:T(8,128)(2,1)S(1)} %get-tuple-element.11.ya_ref, f32[4,8,2,2,256]{4,3,2,1,0:T(2,128)S(1)} %get-tuple-element.12.rbuf_ref, bf16[512,512]{1,0:T(8,128)(2,1)S(1)} %copy-done.1, f32[4,512,128]{2,1,0:T(8,128)S(1)} %get-tuple-element.13.ph), custom_call_target="tpu_custom_call" | custom-call | tf_op jit(solution)/shard_map/adjoint/pallas_call | solution.py:542
  34.9 0.0 copy-done
  34.9 2.3 %image.1 = (bf16[1,64,16384]{2,1,0:T(8,128)(2,1)}, f32[1,2,2,8192]{3,2,1,0:T(2,128)}) custom-call(bf16[64,128]{1,0:T(8,128)(2,1)S(1)} %get-tuple-element.14.sums_ref, bf16[4096,128]{1,0:T(8,128)(2,1)S(1)} %copy-done, f32[4,8,2,2,256]{4,3,2,1,0:T(2,128)S(1)} %get-tuple-element.15.rout_ref), custom_call_target="tpu_custom_call" | custom-call | tf_op jit(solution)/shard_map/image/pallas_call | solution.py:572
Async XLA Ops:
  0.6 17.9 %copy-start.3 = (bf16[128,256]{1,0:T(8,128)(2,1)S(1)}, bf16[128,256]{1,0:T(8,128)(2,1)}, u32[]{:S(2)}) copy-start(bf16[128,256]{1,0:T(8,128)(2,1)} %constant.9.clone.interp_ref) | copy-start | bytes 196612
  0.6 22.9 %copy-start.1 = (bf16[512,512]{1,0:T(8,128)(2,1)S(1)}, bf16[512,512]{1,0:T(8,128)(2,1)}, u32[]{:S(2)}) copy-start(bf16[512,512]{1,0:T(8,128)(2,1)} %constant.11.clone.m2_ref) | copy-start | bytes 1572868
  0.7 17.8 %copy-start.4 = (f32[4,4,2,64]{3,2,1,0:T(2,128)S(1)}, f32[4,4,2,64]{3,2,1,0:T(2,128)}, u32[]{:S(2)}) copy-start(f32[4,4,2,64]{3,2,1,0:T(2,128)} %mu_ref.1) | copy-start | bytes 24580
  0.7 17.8 %copy-start.2 = (s32[3,2,8192]{2,1,0:T(2,128)S(1)}, s32[3,2,8192]{2,1,0:T(2,128)}, u32[]{:S(2)}) copy-start(s32[3,2,8192]{2,1,0:T(2,128)} %uvw_ref.1) | copy-start | bytes 589828
  0.7 17.8 %copy-start.5 = (s32[2]{0:T(128)S(1)}, s32[2]{0:T(128)}, u32[]{:S(2)}) copy-start(s32[2]{0:T(128)} %counts_ref.1) | copy-start | bytes 28
  18.5 16.4 %copy-start = (bf16[4096,128]{1,0:T(8,128)(2,1)S(1)}, bf16[4096,128]{1,0:T(8,128)(2,1)}, u32[]{:S(2)}) copy-start(bf16[4096,128]{1,0:T(8,128)(2,1)} %constant.8.clone.column_hbm.column_ref) | copy-start | bytes 3145732

commit v3 on v2

--- a/solution.py
+++ b/solution.py
@@ -265,15 +265,17 @@
             table = jnp.concatenate(
                 [yall_ref[s, j * width : (j + 1) * width, :] for s in range(nst)], 0
             )
-            picked = jnp.dot(table, pick_u, preferred_element_type=jnp.float32)
-            weights = jnp.dot(interp_ref[...], pick_w, preferred_element_type=jnp.float32)
+            picked = jnp.dot(table, pick_u, preferred_element_type=jnp.float32).astype(jnp.bfloat16)
+            weights = jnp.dot(interp_ref[...], pick_w, preferred_element_type=jnp.float32).astype(
+                jnp.bfloat16
+            )
             w_re, w_im = weights[:K], weights[K:]
             model = []
             for s in range(nst):
                 y_re = picked[s * width : s * width + K]
                 y_im = picked[s * width + K : (s + 1) * width]
-                m_re = jnp.sum(y_re * w_re - y_im * w_im, axis=0, keepdims=True)
-                m_im = jnp.sum(y_re * w_im + y_im * w_re, axis=0, keepdims=True)
+                m_re = jnp.sum((y_re * w_re - y_im * w_im).astype(jnp.float32), axis=0, keepdims=True)
+                m_im = jnp.sum((y_re * w_im + y_im * w_re).astype(jnp.float32), axis=0, keepdims=True)
                 model.append(
                     jnp.concatenate([m_re * cosine + m_im * sine, m_im * cosine - m_re * sine], 0)
                 )
@@ -305,19 +307,20 @@
             for s in range(nst):
                 back = jnp.concatenate([backs[0][s], backs[1][s]], 1)
                 b_re, b_im = back[0:1], back[1:2]
-                g_re = b_re * cosine - b_im * sine
-                g_im = b_im * cosine + b_re * sine
-                terms.append((g_re * w_re + g_im * w_im).astype(jnp.bfloat16))
-                terms.append((g_im * w_re - g_re * w_im).astype(jnp.bfloat16))
-            return lax.dot_general(
-                jnp.concatenate(terms, 0),
-                pick_u,
+                g_re = (b_re * cosine - b_im * sine).astype(jnp.bfloat16)
+                g_im = (b_im * cosine + b_re * sine).astype(jnp.bfloat16)
+                terms.append(g_re * w_re + g_im * w_im)
+                terms.append(g_im * w_re - g_re * w_im)
+            return jnp.concatenate(terms, 0), pick_u
+
+        def two_steps(i, carry):
+            terms, picks = zip(step(2 * i), step(2 * i + 1))
+            acc[j] += lax.dot_general(
+                jnp.concatenate(terms, 1),
+                jnp.concatenate(picks, 1),
                 (((1,), (1,)), ((), ())),
                 preferred_element_type=jnp.float32,
             )
-
-        def two_steps(i, carry):
-            acc[j] += step(2 * i) + step(2 * i + 1)
             return carry
 
         lax.fori_loop(0, trips, two_steps, 0)

time: 37.7 us -> 38 us (level)
    pallas_call x1, Pallas kernels: 5.02 us -> 3.93 us  [body(): pl.pallas_call(functools.partial(visibility_kernel, nst, owned), out_shap...]
    pallas_call x1, Pallas kernels: 11.3 us -> 12.4 us  [body(): pl.pallas_call(functools.partial(adjoint_kernel, nfac, nst, owned), out_s...]
where the time goes in v3:
time: 38 us; the launch traced here: 37.2 us
  Pallas kernels  36.4 us (96%)
  between operations  0.75 us (2%)
    pallas_call x1, Pallas kernels, body(): pl.pallas_call(functools.partial(predict_kernel, nfac, nst, owned), out_s...  17.8 us
    pallas_call x1, Pallas kernels, body(): pl.pallas_call(functools.partial(adjoint_kernel, nfac, nst, owned), out_s...  12.4 us
    pallas_call x1, Pallas kernels, body(): pl.pallas_call(functools.partial(visibility_kernel, nst, owned), out_shap...  3.93 us
    pallas_call x1, Pallas kernels, body(): pl.pallas_call(functools.partial(image_kernel, nst, owned), out_shape=(ja...  2.35 us

profile of v3, /device:TPU:0, one launch (start us, length us, event | category | flops | bytes accessed | tf_op | source)
XLA Modules:
  0.0 37.2 jit_solution(16853410721176975654)
XLA Ops:
  0.6 0.0 copy-start.3
  0.6 0.0 copy-start.1
  0.7 0.0 copy-start.4
  0.7 0.0 copy-start.2
  0.7 0.0 copy-start.5
  0.7 17.8 %predict.1 = (bf16[4,256,256]{2,1,0:T(8,128)(2,1)S(1)}, f32[4,8,2,2,256]{4,3,2,1,0:T(2,128)S(1)}, f32[4,512,128]{2,1,0:T(8,128)S(1)}) custom-call(bf16[1,64,16384]{2,1,0:T(8,128)(2,1)} %strips_hbm.1, bf16[4096,128]{1,0:T(8,128)(2,1)} %constant.8.clone.column_hbm.column_ref, bf16[256,1024]{1,0:T(8,128)(2,1)} %constant.10.clone.m0_hbm, s32[16]{0:T(128)} %offsets_ref.1, ...), custom_call_target="tpu_custom_call" | custom-call | tf_op jit(solution)/shard_map/predict/pallas_call | solution.py:503
  18.5 0.0 copy-start
  18.5 0.0 copy-done.3
  18.5 0.0 copy-done.4
  18.5 0.0 copy-done.2
  18.5 0.0 copy-done.5
  18.5 3.9 %visibility.1 = (f32[4,8,2,2,256]{4,3,2,1,0:T(2,128)S(1)}, bf16[4,256,256]{2,1,0:T(8,128)(2,1)S(1)}) custom-call(s32[2]{0:T(128)S(1)} %copy-done.5, f32[4,4,2,64]{3,2,1,0:T(2,128)S(1)} %copy-done.4, bf16[4,256,256]{2,1,0:T(8,128)(2,1)S(1)} %get-tuple-element.9.yall_ref, bf16[128,256]{1,0:T(8,128)(2,1)S(1)} %copy-done.3, s32[3,2,8192]{2,1,0:T(2,128)S(1)} %copy-done.2, ...), custom_call_target="tpu_custom_call" | custom-call | tf_op jit(solution)/shard_map/visibility/pallas_call | solution.py:532
  22.5 0.0 copy-done.1
  22.5 12.4 %adjoint.1 = (bf16[64,128]{1,0:T(8,128)(2,1)S(1)}, f32[4,8,2,2,256]{4,3,2,1,0:T(2,128)S(1)}) custom-call(bf16[4,256,256]{2,1,0:T(8,128)(2,1)S(1)} %get-tuple-element.11.ya_ref, f32[4,8,2,2,256]{4,3,2,1,0:T(2,128)S(1)} %get-tuple-element.12.rbuf_ref, bf16[512,512]{1,0:T(8,128)(2,1)S(1)} %copy-done.1, f32[4,512,128]{2,1,0:T(8,128)S(1)} %get-tuple-element.13.ph), custom_call_target="tpu_custom_call" | custom-call | tf_op jit(solution)/shard_map/adjoint/pallas_call | solution.py:545
  34.9 0.0 copy-done
  34.9 2.3 %image.1 = (bf16[1,64,16384]{2,1,0:T(8,128)(2,1)}, f32[1,2,2,8192]{3,2,1,0:T(2,128)}) custom-call(bf16[64,128]{1,0:T(8,128)(2,1)S(1)} %get-tuple-element.14.sums_ref, bf16[4096,128]{1,0:T(8,128)(2,1)S(1)} %copy-done, f32[4,8,2,2,256]{4,3,2,1,0:T(2,128)S(1)} %get-tuple-element.15.rout_ref), custom_call_target="tpu_custom_call" | custom-call | tf_op jit(solution)/shard_map/image/pallas_call | solution.py:575
Async XLA Ops:
  0.6 17.9 %copy-start.3 = (bf16[128,256]{1,0:T(8,128)(2,1)S(1)}, bf16[128,256]{1,0:T(8,128)(2,1)}, u32[]{:S(2)}) copy-start(bf16[128,256]{1,0:T(8,128)(2,1)} %constant.9.clone.interp_ref) | copy-start | bytes 196612
  0.6 21.8 %copy-start.1 = (bf16[512,512]{1,0:T(8,128)(2,1)S(1)}, bf16[512,512]{1,0:T(8,128)(2,1)}, u32[]{:S(2)}) copy-start(bf16[512,512]{1,0:T(8,128)(2,1)} %constant.11.clone.m2_ref) | copy-start | bytes 1572868
  0.7 17.8 %copy-start.4 = (f32[4,4,2,64]{3,2,1,0:T(2,128)S(1)}, f32[4,4,2,64]{3,2,1,0:T(2,128)}, u32[]{:S(2)}) copy-start(f32[4,4,2,64]{3,2,1,0:T(2,128)} %mu_ref.1) | copy-start | bytes 24580
  0.7 17.8 %copy-start.2 = (s32[3,2,8192]{2,1,0:T(2,128)S(1)}, s32[3,2,8192]{2,1,0:T(2,128)}, u32[]{:S(2)}) copy-start(s32[3,2,8192]{2,1,0:T(2,128)} %uvw_ref.1) | copy-start | bytes 589828
  0.7 17.8 %copy-start.5 = (s32[2]{0:T(128)S(1)}, s32[2]{0:T(128)}, u32[]{:S(2)}) copy-start(s32[2]{0:T(128)} %counts_ref.1) | copy-start | bytes 28
  18.5 16.4 %copy-start = (bf16[4096,128]{1,0:T(8,128)(2,1)S(1)}, bf16[4096,128]{1,0:T(8,128)(2,1)}, u32[]{:S(2)}) copy-start(bf16[4096,128]{1,0:T(8,128)(2,1)} %constant.8.clone.column_hbm.column_ref) | copy-start | bytes 3145732
